TPU v7x, 128 devices: a whole 4x4x4 slice. The times are simulated.
128 devices in a mesh: row: 8 (over x, core), col: 16 (over z, y).
Axes of the slice: x: 4, y: 4, z: 4, core: 2. Of those that a mesh axis runs over, the one named last changes fastest.
Arguments:
- raw_vectors: float32 [4096, 81920], P('col', 'row'), may hold values from -810 to 810
- interval_count: int32 [16], replicated, may hold values from 1 to 256, 2048 in all
- cluster_of: int32 [16, 256], P('col'), may hold values from 0 to 31, never falling along the last dimension, each value on 1 to 32 neighbouring positions
- panel_one: float32 [81920, 256], P(('row', 'col')), may hold values from -0.03125 to 0.03125
- factor_one: float32 [256, 256], replicated, may hold values from -0.3 to 2
- panel_two: float32 [81920, 256], P(('row', 'col')), may hold values from -0.03125 to 0.03125
- factor_two: float32 [256, 256], replicated, may hold values from -0.3 to 2
Outputs:
- eigenvectors: float32 [2048, 81920], P('col', 'row')
Inputs may be any that keep to these rules, and one draw needn't show every extreme that they name: `interval_count`: the counts sum to 2048; one is exactly 256. `cluster_of`: labels never fall along an interval's slots; one label covers at most 32 slots, and one covers exactly 32.
All inputs are finite; a program needn't handle non-finite values.
Results may differ from a plain program's by a relative error of at most 0.0003.
Values sent between devices are 32-bit elements; how exact they have to be, the bound alone decides.
A program may use at most 128 MiB of HBM per device.

v0:
```python
import math
import jax
import jax.numpy as jnp
from jax import lax
from jax.sharding import PartitionSpec as P

N = 81920
NB = 16
KD = 128
highest = lax.Precision.HIGHEST


def block_order(counts, column_count, per_device, capacity):
    positions = jnp.arange(column_count * per_device, dtype=jnp.int32)
    device_of = positions // per_device
    local_index = positions % per_device
    rank_of = (local_index // NB * column_count + device_of) * NB + local_index % NB
    interval_end = jnp.cumsum(counts)
    interval_start = interval_end - counts
    owner_device = jnp.sum((interval_end[None, :] <= rank_of[:, None]).astype(jnp.int32), axis=1)
    owner_hit = jnp.arange(column_count, dtype=jnp.int32)[None, :] == owner_device[:, None]
    owner_start = jnp.sum(jnp.where(owner_hit, interval_start[None, :], 0), axis=1)
    return owner_device * capacity + rank_of - owner_start


def finish_block(gram_full, raw_block, labels, is_alive):
    same_group = (labels[:, None] == labels[None, :]) & is_alive[:, None] & is_alive[None, :]
    alive_float = is_alive.astype(jnp.float32)
    masked = jnp.where(same_group, gram_full, 0.0) + jnp.diag(1.0 - alive_float)
    lower_factor = jnp.linalg.cholesky(masked)
    solved = jax.scipy.linalg.solve_triangular(lower_factor, raw_block, lower=True)
    return solved * math.sqrt(N)


def apply_panel(vectors, projected, reflectors, factor):
    scaled = jnp.dot(projected, factor.T, precision=highest, preferred_element_type=jnp.float32)
    return vectors - jnp.einsum("kr,nr->kn", scaled, reflectors, precision=highest)


def project_sum(partial_terms):
    return lax.psum(partial_terms, "row")


def transform(vectors, reflect_one, factor_one, reflect_two, factor_two):
    for reflectors, factor in ((reflect_two, factor_two), (reflect_one, factor_one)):
        partial_terms = jnp.dot(
            vectors, reflectors, precision=highest, preferred_element_type=jnp.float32
        )
        projected = project_sum(partial_terms)
        vectors = apply_panel(vectors, projected, reflectors, factor)
    return vectors


def regroup(vectors):
    return lax.all_to_all(vectors, "col", split_axis=0, concat_axis=1, tiled=True)


def sectioned_order(orthogonal, interval_count, column_count, capacity):
    spread = lax.all_to_all(orthogonal, "col", split_axis=1, concat_axis=0, tiled=True)
    wanted = block_order(interval_count, column_count, KD, capacity)
    return jnp.take(spread, wanted, axis=0)


def body(raw_vectors, interval_count, cluster_of, panel_one, factor_one, panel_two, factor_two):
    column_count = lax.axis_size("col")
    column_index = lax.axis_index("col")
    capacity = raw_vectors.shape[0]
    own_hit = jnp.arange(column_count, dtype=jnp.int32) == column_index
    own_count = jnp.sum(jnp.where(own_hit, interval_count, 0))
    is_alive = jnp.arange(capacity, dtype=jnp.int32) < own_count
    gram_part = jnp.dot(
        raw_vectors, raw_vectors.T, precision=highest, preferred_element_type=jnp.float32
    )
    gram_full = lax.psum(gram_part, "row")
    orthogonal = finish_block(gram_full, raw_vectors, cluster_of[0], is_alive)
    local_rows = regroup(sectioned_order(orthogonal, interval_count, column_count, capacity))
    full_one, full_two = (
        lax.all_gather(panel_one, "col", axis=0, tiled=True),
        lax.all_gather(panel_two, "col", axis=0, tiled=True),
    )
    return transform(local_rows, full_one, factor_one, full_two, factor_two)


def solution(mesh):
    placed = (
        P("col", "row"),
        P(),
        P("col", None),
        P(("row", "col"), None),
        P(),
        P(("row", "col"), None),
        P(),
    )
    return jax.shard_map(
        body, mesh=mesh, in_specs=placed, out_specs=P("col", "row"), check_vma=False
    )
```

profile of v0, /device:TPU:0, one launch (start us, length us, event | category | flops | bytes accessed | tf_op | source)
XLA Modules:
  0.0 624.0 jit_solution(3389111985791579401)
XLA Ops:
  7.4 12.7 %fusion.50 = f32[256,256]{0,1:T(8,128)} fusion(f32[256,10240]{1,0:T(8,128)} %param.7), kind=kOutput, calls=%fused_computation.117 | convolution fusion | flops 8053063680 | bytes 10747904 | tf_op jit(solution)/shard_map/dot_general | solution.py:71
  23.1 61.2 %all-reduce.5.cloned.1.call-done = f32[256,256]{0,1:T(8,128)} async-done(((f32[256,256]{0,1:T(8,128)}), f32[256,256]{0,1:T(8,128)}) %all-reduce.5.cloned.1.call-update) | async-done | bytes 262160 | tf_op jit(solution)/shard_map/psum | solution.py:74
  85.5 1.1 fusion.3
  86.6 11.7 %cholesky.49 = f32[128,128]{1,0:T(8,128)S(1)} custom-call(f32[128,128]{1,0:T(8,128)S(1)} %cholesky.115), custom_call_target="Cholesky" | custom-call | tf_op jit(solution)/shard_map/jit(cholesky)/cholesky | solution.py:30
  98.4 9.8 %custom-call.15 = f32[1,128,128]{1,2,0:T(8,128)S(1)} custom-call(f32[1,128,128]{2,1,0:T(8,128)S(1)} %get-tuple-element.40), custom_call_target="InvertDiagBlocksLowerTriangular" | custom-call | tf_op jit(solution)/shard_map/jit(cholesky)/cholesky | solution.py:30
  108.8 11.7 %cholesky.103 = f32[128,128]{1,0:T(8,128)S(1)} custom-call(f32[128,128]{1,0:T(8,128)S(1)} %convolution_subtract_fusion.3), custom_call_target="Cholesky" | custom-call | tf_op jit(solution)/shard_map/jit(cholesky)/cholesky | solution.py:30
  122.9 4.4 while.1
  123.7 1.4 dynamic-slice.7
  125.8 1.4 dynamic-slice.7
  127.3 19.7 %custom-call.16 = f32[2,128,128]{1,2,0:T(8,128)S(1)} custom-call(f32[2,128,128]{2,1,0:T(8,128)S(1)} %get-tuple-element.12), custom_call_target="InvertDiagBlocksLowerTriangular" | custom-call | tf_op jit(solution)/shard_map/jit(_solve_triangular)/triangular_solve | solution.py:31
  147.0 6.8 %fusion.1 = f32[128,10240]{1,0:T(8,128)S(1)} fusion(f32[256,10240]{1,0:T(8,128)} %param.7, f32[2,128,128]{1,2,0:T(8,128)S(1)} %custom-call.16), kind=kOutput, calls=%fused_computation.9 | convolution fusion | flops 2013265920 | bytes 10551296 | tf_op jit(solution)/shard_map/jit(_solve_triangular)/triangular_solve | solution.py:31
  153.8 2.2 copy-done.2
  156.1 6.4 %fusion = f32[10240,128]{0,1:T(8,128)} fusion(f32[128,10240]{1,0:T(8,128)S(1)} %fusion.1, f32[256,10240]{1,0:T(8,128)S(1)} %copy-done.1, f32[256,256]{0,1:T(8,128)S(1)} %get-tuple-element.98), kind=kOutput, calls=%fused_computation.6 | convolution fusion | flops 2014576640 | bytes 15794176 | tf_op jit(solution)/shard_map/jit(_solve_triangular)/triangular_solve | solution.py:31
  162.5 5.9 copy.56
  168.4 5.5 copy.61
  173.9 6.3 %fusion.5 = f32[128,16,640]{2,0,1:T(8,128)} fusion(f32[16,640,128]{2,1,0:T(8,128)S(1)} %bitcast.76, f32[2,128,128]{1,2,0:T(8,128)S(1)} %custom-call.16), kind=kOutput, calls=%fused_computation.24 | convolution fusion | flops 2013265920 | bytes 10551296 | tf_op jit(solution)/shard_map/jit(_solve_triangular)/triangular_solve | solution.py:31
  180.1 9.0 %maximum_multiply_fusion = f32[256,16,640]{2,0,1:T(8,128)} fusion(f32[128,16,640]{2,0,1:T(8,128)} %fusion.5, f32[128,16,640]{2,0,1:T(8,128)} %bitcast.75), kind=kLoop, calls=%fused_computation.7 | loop fusion | flops 5242880 | bytes 20971520 | tf_op jit(solution)/shard_map/mul | solution.py:32
  189.1 6.8 %all-to-all-start = ((f32[256,16,640]{2,0,1:T(8,128)}), f32[256,16,640]{2,0,1:T(8,128)}, u32[]{:S(2)}, u32[]{:S(2)}) async-start(f32[256,16,640]{2,0,1:T(8,128)} %maximum_multiply_fusion), calls=%async_computation | async-start | bytes 20971520 | tf_op jit(solution)/shard_map/all_to_all | solution.py:59
  196.3 149.8 %all-to-all-done = f32[256,16,640]{2,0,1:T(8,128)} async-done(((f32[256,16,640]{2,0,1:T(8,128)}), f32[256,16,640]{2,0,1:T(8,128)}, u32[]{:S(2)}, u32[]{:S(2)}) %all-to-all-start) | async-done | bytes 10485792 | tf_op jit(solution)/shard_map/all_to_all | solution.py:59
  346.1 14.1 %gather_fusion = f32[2048,640]{1,0:T(8,128)} fusion(f32[4096,640]{1,0:T(8,128)} %bitcast.13, s32[2048]{0:T(1024)S(1)} %broadcast_clamp_fusion), kind=kCustom, calls=%fused_computation | custom fusion | bytes 10493952 | tf_op jit(solution)/shard_map/jit(_take)/gather | solution.py:61
  360.2 2.8 broadcast_select_fusion
  363.0 63.6 %all_to_all.32 = f32[16,128,640]{2,1,0:T(8,128)S(1)} all-to-all(f32[16,128,640]{2,1,0:T(8,128)S(1)} %broadcast_select_fusion), channel_id=1, replica_groups=mesh['row'=8,'col'=16] {'col'}, dimensions={0} | all-to-all | bytes 10485760 | tf_op jit(solution)/shard_map/all_to_all | solution.py:55
  426.5 2.9 copy.59
  429.4 9.2 %fusion.51 = f32[128,256]{1,0:T(8,128)} fusion(f32[128,10240]{1,0:T(8,128)} %bitcast.72, f32[10240,256]{1,0:T(8,128)} %all-gather.3.cloned.1.call-done), kind=kOutput, calls=%fused_computation.118 | convolution fusion | flops 4026531840 | bytes 15859712 | tf_op jit(solution)/shard_map/dot_general | solution.py:46
  439.3 66.5 %all-reduce.7.cloned.1.call-done = f32[128,256]{1,0:T(8,128)} async-done(((f32[128,256]{1,0:T(8,128)}), f32[128,256]{1,0:T(8,128)}) %all-reduce.7.cloned.1.call-update) | async-done | bytes 131088 | tf_op jit(solution)/shard_map/psum | solution.py:41
  505.8 1.3 fusion.52
  507.1 18.8 %convolution_subtract_fusion.1 = f32[128,10240]{1,0:T(8,128)} fusion(f32[128,10240]{1,0:T(8,128)} %bitcast.73, f32[128,256]{1,0:T(8,128)S(1)} %fusion.52, f32[10240,256]{1,0:T(8,128)} %all-gather.3.cloned.1.call-done), kind=kOutput, calls=%fused_computation.4 | convolution fusion | flops 4027842560 | bytes 21102592 | tf_op jit(solution)/shard_map/kr,nr->kn/dot_general | solution.py:37
  525.9 1.7 all-gather.5.cloned.1.call-done
  527.6 9.5 %fusion.53 = f32[128,256]{1,0:T(8,128)} fusion(f32[128,10240]{1,0:T(8,128)} %convolution_subtract_fusion.1, f32[10240,256]{1,0:T(8,128)} %all-gather.5.cloned.1.call-done), kind=kOutput, calls=%fused_computation.120 | convolution fusion | flops 4026531840 | bytes 15859712 | tf_op jit(solution)/shard_map/dot_general | solution.py:46
  537.1 59.6 %all-reduce.9.cloned.1.call-done = f32[128,256]{1,0:T(8,128)} async-done(((f32[128,256]{1,0:T(8,128)}), f32[128,256]{1,0:T(8,128)}) %all-reduce.9.cloned.1.call-update) | async-done | bytes 131088 | tf_op jit(solution)/shard_map/psum | solution.py:41
  596.7 1.3 fusion.54
  598.0 18.4 %convolution_subtract_fusion = f32[128,10240]{1,0:T(8,128)} fusion(f32[128,10240]{1,0:T(8,128)} %convolution_subtract_fusion.1, f32[128,256]{1,0:T(8,128)S(1)} %fusion.54, f32[10240,256]{1,0:T(8,128)} %all-gather.5.cloned.1.call-done), kind=kOutput, calls=%fused_computation.3 | convolution fusion | flops 4027842560 | bytes 21102592 | tf_op jit(solution)/shard_map/kr,nr->kn/dot_general | solution.py:37
  (63 shorter events, 8.2 us)
Async XLA Ops:
  7.4 498.4 %copy-start = (f32[256,256]{1,0:T(8,128)S(1)}, f32[256,256]{1,0:T(8,128)}, u32[]{:S(2)}) copy-start(f32[256,256]{1,0:T(8,128)} %param.13) | copy-start | bytes 786436
  7.4 13.3 %copy-start.6 = (s32[16]{0:T(128)S(1)}, s32[16]{0:T(128)}, u32[]{:S(2)}) copy-start(s32[16]{0:T(128)} %param.8) | copy-start | bytes 196
  7.4 76.9 %copy-start.5 = (s32[1,256]{1,0:T(1,128)S(1)}, s32[1,256]{1,0:T(1,128)}, u32[]{:S(2)}) copy-start(s32[1,256]{1,0:T(1,128)} %param.9) | copy-start | bytes 3076
  7.4 76.9 %all-reduce.5.cloned.1.call-start = ((), (), s32[]{:S(2)}) async-start(), calls=%async_computation.2 | async-start | bytes 524288 | tf_op jit(solution)/shard_map/psum | solution.py:74
  20.1 409.3 %all-gather.3.cloned.1.call-start = ((), (), s32[]{:S(2)}) async-start(), calls=%async_computation.3 | async-start | bytes 11141120 | tf_op jit(solution)/shard_map/all_gather | solution.py:79
  147.0 9.1 %copy-start.1 = (f32[256,10240]{1,0:T(8,128)S(1)}, f32[256,10240]{1,0:T(8,128)}, u32[]{:S(2)}) copy-start(f32[256,10240]{1,0:T(8,128)} %param.7) | copy-start | bytes 31457284
  153.8 2.2 copy-start.2
  168.4 5.5 copy-start.3
  189.1 157.0 %all-to-all-start = ((f32[256,16,640]{2,0,1:T(8,128)}), f32[256,16,640]{2,0,1:T(8,128)}, u32[]{:S(2)}, u32[]{:S(2)}) async-start(f32[256,16,640]{2,0,1:T(8,128)} %maximum_multiply_fusion), calls=%async_computation | async-start | bytes 20971520 | tf_op jit(solution)/shard_map/all_to_all | solution.py:59
  195.9 309.9 %all-reduce.7.cloned.1.call-start = ((), (), s32[]{:S(2)}) async-start(), calls=%async_computation.4 | async-start | bytes 262144 | tf_op jit(solution)/shard_map/psum | solution.py:41
  438.7 89.0 %all-gather.5.cloned.1.call-start = ((), (), s32[]{:S(2)}) async-start(), calls=%async_computation.5 | async-start | bytes 11141120 | tf_op jit(solution)/shard_map/all_gather | solution.py:78
  439.3 157.4 %all-reduce.9.cloned.1.call-start = ((), (), s32[]{:S(2)}) async-start(), calls=%async_computation.6 | async-start | bytes 262144 | tf_op jit(solution)/shard_map/psum | solution.py:41
  525.9 70.8 %copy-start.4 = (f32[256,256]{1,0:T(8,128)S(1)}, f32[256,256]{1,0:T(8,128)}, u32[]{:S(2)}) copy-start(f32[256,256]{1,0:T(8,128)} %param.11) | copy-start | bytes 786436
Sparse Core Ops, SparseCore 0:
  20.2 63.9 all-reduce.4
  438.8 66.9 all-reduce.6
  537.3 59.3 all-reduce.8
Sparse Core Ops, SparseCore 1:
  22.7 83.0 all-gather.2
  441.3 86.3 all-gather.4
where the time goes:
time: 627 us; the launch traced here: 624 us
  waiting for transfers between devices  339 us (54%)
  matrix products  91.2 us (15%)
  other arithmetic  70.2 us (11%)
  blocking collectives  63.6 us (10%)
  local copies, waits for them, and re-layouts  35.4 us (6%)
  between operations  16.6 us (3%)
  starting transfers between devices  7.52 us (1%)
    all_to_all x1, waiting for transfers between devices, sectioned_order(): lax.all_to_all(orthogonal, 'col', split_axis=1, concat_axis=0, tiled=True)  150 us
    psum x2, waiting for transfers between devices, project_sum(): return lax.psum(partial_terms, 'row')  126 us
    all_to_all x1, blocking collectives, regroup(): lax.all_to_all(vectors, 'col', split_axis=0, concat_axis=1, tiled=True)  63.6 us
    psum x1, waiting for transfers between devices, body(): gram_full = lax.psum(gram_part, 'row')  61.2 us
    dot_general x2, matrix products, apply_panel(): jnp.einsum('kr,nr->kn', scaled, reflectors, precision=highest)  37.3 us
    another operation x6, other arithmetic, finish_block(): lower_factor = jnp.linalg.cholesky(masked)  34 us
    another operation x3, other arithmetic, finish_block(): jax.scipy.linalg.solve_triangular(lower_factor, raw_block, lower=True)  19.7 us
    another operation x3, matrix products, finish_block(): jax.scipy.linalg.solve_triangular(lower_factor, raw_block, lower=True)  19.5 us
  transfers between devices with their start and end apart: 6, of which 5 were waited for; matrix products, arithmetic and copies ran while one was open for 23% of the time, Pallas kernels for 0%

commit v1 on v0

--- a/solution.py
+++ b/solution.py
@@ -71,7 +71,7 @@
     gram_part = jnp.dot(
         raw_vectors, raw_vectors.T, precision=highest, preferred_element_type=jnp.float32
     )
-    gram_full = lax.psum(gram_part, "row")
+    gram_full = jnp.sum(lax.all_gather(gram_part, "row"), axis=0)
     orthogonal = finish_block(gram_full, raw_vectors, cluster_of[0], is_alive)
     local_rows = regroup(sectioned_order(orthogonal, interval_count, column_count, capacity))
     full_one, full_two = (

time: 627 us -> 649 us (1.035)
  waiting for transfers between devices: 339 us -> 360 us
    psum x1 -> x0, waiting for transfers between devices: 61.2 us -> none  [body(): gram_full = lax.psum(gram_part, 'row')]
    all_gather x1, waiting for transfers between devices: 1.72 us -> 61.7 us  [body(): lax.all_gather(panel_one, 'col', axis=0, tiled=True)]
    all_gather x0 -> x1, waiting for transfers between devices: none -> 24.8 us  [body(): gram_full = jnp.sum(lax.all_gather(gram_part, 'row'), axis=0)]
    psum x2, waiting for transfers between devices: 126 us -> 115 us  [project_sum(): return lax.psum(partial_terms, 'row')]
    all_to_all x1, waiting for transfers between devices: 150 us -> 157 us  [sectioned_order(): lax.all_to_all(orthogonal, 'col', split_axis=1, concat_axis=0, tiled=True)]
  transfers between devices with their start and end apart: 6 -> 6, of which waited for: 5 -> 5; matrix products, arithmetic and copies ran while one was open for 23% -> 22% of each run, Pallas kernels for 0% -> 0%
where the time goes in v1:
time: 649 us; the launch traced here: 644 us
  waiting for transfers between devices  360 us (55%)
  matrix products  91.6 us (14%)
  other arithmetic  70 us (11%)
  blocking collectives  65.5 us (10%)
  local copies, waits for them, and re-layouts  35.1 us (5%)
  between operations  14.9 us (2%)
  starting transfers between devices  7.31 us (1%)
    all_to_all x1, waiting for transfers between devices, sectioned_order(): lax.all_to_all(orthogonal, 'col', split_axis=1, concat_axis=0, tiled=True)  157 us
    psum x2, waiting for transfers between devices, project_sum(): return lax.psum(partial_terms, 'row')  115 us
    all_to_all x1, blocking collectives, regroup(): lax.all_to_all(vectors, 'col', split_axis=0, concat_axis=1, tiled=True)  65.5 us
    all_gather x1, waiting for transfers between devices, body(): lax.all_gather(panel_one, 'col', axis=0, tiled=True)  61.7 us
    dot_general x2, matrix products, apply_panel(): jnp.einsum('kr,nr->kn', scaled, reflectors, precision=highest)  36.9 us
    another operation x6, other arithmetic, finish_block(): lower_factor = jnp.linalg.cholesky(masked)  34 us
    all_gather x1, waiting for transfers between devices, body(): gram_full = jnp.sum(lax.all_gather(gram_part, 'row'), axis=0)  24.8 us
    another operation x3, other arithmetic, finish_block(): jax.scipy.linalg.solve_triangular(lower_factor, raw_block, lower=True)  19.7 us
  transfers between devices with their start and end apart: 6, of which 5 were waited for; matrix products, arithmetic and copies ran while one was open for 22% of the time, Pallas kernels for 0%

profile of v1, /device:TPU:0, one launch (start us, length us, event | category | flops | bytes accessed | tf_op | source)
XLA Modules:
  0.0 644.1 jit_solution(2422682928386055619)
XLA Ops:
  6.5 13.6 %fusion.52 = f32[256,256]{1,0:T(8,128)} fusion(f32[256,10240]{1,0:T(8,128)} %param.7), kind=kOutput, calls=%fused_computation.119 | convolution fusion | flops 8053063680 | bytes 10747904 | tf_op jit(solution)/shard_map/dot_general | solution.py:71
  23.2 24.8 %all-gather.9.cloned.1.call-done = f32[2048,256]{1,0:T(8,128)} async-done(((f32[256,256]{1,0:T(8,128)}), f32[2048,256]{1,0:T(8,128)}) %all-gather.9.cloned.1.call-update) | async-done | bytes 2097168 | tf_op jit(solution)/shard_map/all_gather | solution.py:74
  48.1 1.8 reduce_sum.46
  50.2 11.7 %cholesky.49 = f32[128,128]{1,0:T(8,128)S(1)} custom-call(f32[128,128]{1,0:T(8,128)S(1)} %cholesky.115), custom_call_target="Cholesky" | custom-call | tf_op jit(solution)/shard_map/jit(cholesky)/cholesky | solution.py:30
  62.0 9.8 %custom-call.15 = f32[1,128,128]{1,2,0:T(8,128)S(1)} custom-call(f32[1,128,128]{2,1,0:T(8,128)S(1)} %get-tuple-element.26), custom_call_target="InvertDiagBlocksLowerTriangular" | custom-call | tf_op jit(solution)/shard_map/jit(cholesky)/cholesky | solution.py:30
  72.3 11.7 %cholesky.103 = f32[128,128]{1,0:T(8,128)S(1)} custom-call(f32[128,128]{1,0:T(8,128)S(1)} %convolution_subtract_fusion.3), custom_call_target="Cholesky" | custom-call | tf_op jit(solution)/shard_map/jit(cholesky)/cholesky | solution.py:30
  86.2 4.2 while.1
  87.0 1.4 bitcast_dynamic-update-slice_fusion.2
  89.0 1.4 bitcast_dynamic-update-slice_fusion.2
  90.4 19.7 %custom-call.16 = f32[2,128,128]{1,2,0:T(8,128)S(1)} custom-call(f32[2,128,128]{2,1,0:T(8,128)S(1)} %get-tuple-element.12), custom_call_target="InvertDiagBlocksLowerTriangular" | custom-call | tf_op jit(solution)/shard_map/jit(_solve_triangular)/triangular_solve | solution.py:31
  110.1 6.9 %fusion.1 = f32[128,10240]{1,0:T(8,128)S(1)} fusion(f32[256,10240]{1,0:T(8,128)} %param.7, f32[2,128,128]{1,2,0:T(8,128)S(1)} %custom-call.16), kind=kOutput, calls=%fused_computation.9 | convolution fusion | flops 2013265920 | bytes 10551296 | tf_op jit(solution)/shard_map/jit(_solve_triangular)/triangular_solve | solution.py:31
  117.0 2.2 copy-done.2
  119.2 6.3 fusion
  125.6 5.9 copy.41
  131.4 5.5 copy.45
  136.9 6.3 fusion.7
  143.2 9.0 %maximum_multiply_fusion = f32[256,16,640]{2,0,1:T(8,128)} fusion(f32[128,16,640]{2,0,1:T(8,128)} %fusion.7, f32[128,16,640]{2,0,1:T(8,128)} %bitcast.82), kind=kLoop, calls=%fused_computation.7 | loop fusion | flops 5242880 | bytes 20971520 | tf_op jit(solution)/shard_map/mul | solution.py:32
  152.1 7.0 %all-to-all-start = ((f32[256,16,640]{2,0,1:T(8,128)}), f32[256,16,640]{2,0,1:T(8,128)}, u32[]{:S(2)}, u32[]{:S(2)}) async-start(f32[256,16,640]{2,0,1:T(8,128)} %maximum_multiply_fusion), calls=%async_computation | async-start | bytes 20971520 | tf_op jit(solution)/shard_map/all_to_all | solution.py:59
  159.5 156.8 %all-to-all-done = f32[256,16,640]{2,0,1:T(8,128)} async-done(((f32[256,16,640]{2,0,1:T(8,128)}), f32[256,16,640]{2,0,1:T(8,128)}, u32[]{:S(2)}, u32[]{:S(2)}) %all-to-all-start) | async-done | bytes 10485792 | tf_op jit(solution)/shard_map/all_to_all | solution.py:59
  316.3 14.3 %gather_fusion = f32[2048,640]{1,0:T(8,128)} fusion(f32[4096,640]{1,0:T(8,128)} %bitcast.14, s32[2048]{0:T(1024)S(1)} %broadcast_clamp_fusion), kind=kCustom, calls=%fused_computation | custom fusion | bytes 10493952 | tf_op jit(solution)/shard_map/jit(_take)/gather | solution.py:61
  330.6 2.8 broadcast_select_fusion
  333.4 65.5 %all_to_all.32 = f32[16,128,640]{2,1,0:T(8,128)S(1)} all-to-all(f32[16,128,640]{2,1,0:T(8,128)S(1)} %broadcast_select_fusion), channel_id=1, replica_groups=mesh['row'=8,'col'=16] {'col'}, dimensions={0} | all-to-all | bytes 10485760 | tf_op jit(solution)/shard_map/all_to_all | solution.py:55
  398.9 2.9 copy.43
  401.8 9.2 %fusion.53 = f32[128,256]{1,0:T(8,128)} fusion(f32[128,10240]{1,0:T(8,128)} %bitcast.79, f32[10240,256]{1,0:T(8,128)} %all-gather.5.cloned.1.call-done), kind=kOutput, calls=%fused_computation.120 | convolution fusion | flops 4026531840 | bytes 15859712 | tf_op jit(solution)/shard_map/dot_general | solution.py:46
  411.6 55.6 %all-reduce.4.cloned.1.call-done = f32[128,256]{1,0:T(8,128)} async-done(((f32[128,256]{1,0:T(8,128)}), f32[128,256]{1,0:T(8,128)}) %all-reduce.4.cloned.1.call-update) | async-done | bytes 131088 | tf_op jit(solution)/shard_map/psum | solution.py:41
  467.2 1.3 fusion.54
  468.5 18.4 %convolution_subtract_fusion.1 = f32[128,10240]{1,0:T(8,128)} fusion(f32[128,10240]{1,0:T(8,128)} %bitcast.80, f32[128,256]{1,0:T(8,128)S(1)} %fusion.54, f32[10240,256]{1,0:T(8,128)} %all-gather.5.cloned.1.call-done), kind=kOutput, calls=%fused_computation.4 | convolution fusion | flops 4027842560 | bytes 21102592 | tf_op jit(solution)/shard_map/kr,nr->kn/dot_general | solution.py:37
  486.9 61.7 %all-gather.7.cloned.1.call-done = f32[10240,256]{1,0:T(8,128)} async-done(((f32[640,256]{1,0:T(8,128)}), f32[10240,256]{1,0:T(8,128)}) %all-gather.7.cloned.1.call-update) | async-done | bytes 10485776 | tf_op jit(solution)/shard_map/all_gather | solution.py:78
  548.7 9.4 %fusion.55 = f32[128,256]{1,0:T(8,128)} fusion(f32[128,10240]{1,0:T(8,128)} %convolution_subtract_fusion.1, f32[10240,256]{1,0:T(8,128)} %all-gather.7.cloned.1.call-done), kind=kOutput, calls=%fused_computation.122 | convolution fusion | flops 4026531840 | bytes 15859712 | tf_op jit(solution)/shard_map/dot_general | solution.py:46
  558.1 59.6 %all-reduce.6.cloned.1.call-done = f32[128,256]{1,0:T(8,128)} async-done(((f32[128,256]{1,0:T(8,128)}), f32[128,256]{1,0:T(8,128)}) %all-reduce.6.cloned.1.call-update) | async-done | bytes 131088 | tf_op jit(solution)/shard_map/psum | solution.py:41
  617.7 1.3 fusion.56
  619.0 18.4 %convolution_subtract_fusion = f32[128,10240]{1,0:T(8,128)} fusion(f32[128,10240]{1,0:T(8,128)} %convolution_subtract_fusion.1, f32[128,256]{1,0:T(8,128)S(1)} %fusion.56, f32[10240,256]{1,0:T(8,128)} %all-gather.7.cloned.1.call-done), kind=kOutput, calls=%fused_computation.3 | convolution fusion | flops 4027842560 | bytes 21102592 | tf_op jit(solution)/shard_map/kr,nr->kn/dot_general | solution.py:37
  (54 shorter events, 7.0 us)
Async XLA Ops:
  6.5 460.7 %copy-start = (f32[256,256]{1,0:T(8,128)S(1)}, f32[256,256]{1,0:T(8,128)}, u32[]{:S(2)}) copy-start(f32[256,256]{1,0:T(8,128)} %param.13) | copy-start | bytes 786436
  6.5 14.4 %copy-start.6 = (s32[16]{0:T(128)S(1)}, s32[16]{0:T(128)}, u32[]{:S(2)}) copy-start(s32[16]{0:T(128)} %param.8) | copy-start | bytes 196
  6.5 43.4 %copy-start.5 = (s32[1,256]{1,0:T(1,128)S(1)}, s32[1,256]{1,0:T(1,128)}, u32[]{:S(2)}) copy-start(s32[1,256]{1,0:T(1,128)} %param.9) | copy-start | bytes 3076
  6.5 41.5 %all-gather.9.cloned.1.call-start = ((), (), s32[]{:S(2)}) async-start(), calls=%async_computation.6 | async-start | bytes 2359296 | tf_op jit(solution)/shard_map/all_gather | solution.py:74
  20.1 381.6 %all-gather.5.cloned.1.call-start = ((), (), s32[]{:S(2)}) async-start(), calls=%async_computation.2 | async-start | bytes 11141120 | tf_op jit(solution)/shard_map/all_gather | solution.py:79
  110.1 9.1 %copy-start.1 = (f32[256,10240]{1,0:T(8,128)S(1)}, f32[256,10240]{1,0:T(8,128)}, u32[]{:S(2)}) copy-start(f32[256,10240]{1,0:T(8,128)} %param.7) | copy-start | bytes 31457284
  117.0 2.2 copy-start.2
  131.4 5.5 copy-start.3
  152.1 164.1 %all-to-all-start = ((f32[256,16,640]{2,0,1:T(8,128)}), f32[256,16,640]{2,0,1:T(8,128)}, u32[]{:S(2)}, u32[]{:S(2)}) async-start(f32[256,16,640]{2,0,1:T(8,128)} %maximum_multiply_fusion), calls=%async_computation | async-start | bytes 20971520 | tf_op jit(solution)/shard_map/all_to_all | solution.py:59
  159.1 308.1 %all-reduce.4.cloned.1.call-start = ((), (), s32[]{:S(2)}) async-start(), calls=%async_computation.3 | async-start | bytes 262144 | tf_op jit(solution)/shard_map/psum | solution.py:41
  411.0 137.7 %all-gather.7.cloned.1.call-start = ((), (), s32[]{:S(2)}) async-start(), calls=%async_computation.4 | async-start | bytes 11141120 | tf_op jit(solution)/shard_map/all_gather | solution.py:78
  411.6 206.1 %all-reduce.6.cloned.1.call-start = ((), (), s32[]{:S(2)}) async-start(), calls=%async_computation.5 | async-start | bytes 262144 | tf_op jit(solution)/shard_map/psum | solution.py:41
  486.9 130.7 %copy-start.4 = (f32[256,256]{1,0:T(8,128)S(1)}, f32[256,256]{1,0:T(8,128)}, u32[]{:S(2)}) copy-start(f32[256,256]{1,0:T(8,128)} %param.11) | copy-start | bytes 786436
Sparse Core Ops, SparseCore 0:
  20.3 27.7 all-gather.8
  50.2 81.0 all-gather.4
  411.1 56.0 all-reduce.3
  469.2 79.4 all-gather.6
  558.2 59.4 all-reduce.5
